TPU v7x, 128 devices: a whole 4x4x4 slice. The times are simulated.
128 devices in a mesh: pair: 2 (over core), virt: 64 (over z, y, x).
Axes of the slice: x: 4, y: 4, z: 4, core: 2. Of those that a mesh axis runs over, the one named last changes fastest.
Arguments:
- amplitudes: bfloat16 [512, 32768], P('virt', 'pair'), may hold values from -6 to 6
- integrals: bfloat16 [32768, 32768], P('virt', 'pair'), may hold values from -0.03125 to 0.03125
- cycle_integrals: bfloat16 [16384, 16384], P('pair', 'virt'), may hold values from -0.125 to 0.125
- virt_count: int32 [8], replicated, may hold values from 32 to 64, as said below
Outputs:
- ladder: bfloat16 [512, 32768], P(None, 'virt')
- cycle: bfloat16 [8192, 16384], P('pair', 'virt')
Inputs may be any that keep to these rules, and one draw needn't show every extreme that they name: `virt_count`: every irrep keeps at least half of its 64 slots; some irrep has all 64 and some has exactly half.
All inputs are finite; a program needn't handle non-finite values.
Results may differ from a plain program's by a relative error of at most 0.0049.
Values may be sent and summed in bfloat16 or wider, within the bound.
No kernel may reach another device: no remote copies, remote signals or barrier semaphores. Data moves between devices by JAX's collectives and lax.ppermute only.
A program may use at most 256 MiB of HBM per device.

v0:
```python
import jax
import jax.numpy as jnp
from jax import lax
from jax.sharding import PartitionSpec as P

VH = 64
OI = 16
OJ = 32


def irrep_sizes(virt_count, irrep_of):
    irrep_ids = jnp.arange(virt_count.shape[0], dtype=jnp.int32)
    return jnp.sum(
        jnp.where(irrep_of[:, None] == irrep_ids[None, :], virt_count[None, :], 0), axis=1
    )


def pair_mask(virt_count, first_pos, length, slot_width):
    position = first_pos + jnp.arange(length, dtype=jnp.int32)
    irrep_of = position // (slot_width * slot_width)
    slot_one = position // slot_width % slot_width
    slot_two = position % slot_width
    irrep_size = irrep_sizes(virt_count, irrep_of)
    return ((slot_one < irrep_size) & (slot_two < irrep_size)).astype(jnp.float32)


def slot_mask(virt_count, first_pos, length, slot_width):
    position = (first_pos + jnp.arange(length, dtype=jnp.int32)) % (
        virt_count.shape[0] * slot_width
    )
    irrep_of = position // slot_width
    slot_ids = position % slot_width
    return (slot_ids < irrep_sizes(virt_count, irrep_of)).astype(jnp.float32)


def body(amplitudes, integrals, cycle_integrals, virt_count):
    slot_width = VH
    irrep_total = virt_count.shape[0]
    group_width = irrep_total * slot_width
    pair_devs = lax.axis_size("pair")
    ab_count = integrals.shape[0]
    cd_count = integrals.shape[1]
    jb_count = cycle_integrals.shape[1]
    cd_first = lax.axis_index("pair") * cd_count
    ab_first = lax.axis_index("virt") * ab_count
    a_count = ab_count // slot_width
    per_irrep = slot_width * slot_width // ab_count
    masked = amplitudes * pair_mask(virt_count, cd_first, cd_count, slot_width)[None, :].astype(
        jnp.bfloat16
    )
    partial_sums = lax.dot_general(
        lax.all_gather(masked, "virt", axis=0, tiled=True),
        integrals,
        (((1,), (1,)), ((), ())),
        preferred_element_type=jnp.float32,
    )
    keep_pairs = pair_mask(virt_count, ab_first, ab_count, slot_width)[None, :]
    ladder_total = lax.psum(partial_sums, "pair")
    ladder = (ladder_total * keep_pairs).astype(jnp.bfloat16)
    keep_cols = slot_mask(virt_count, lax.axis_index("virt") * jb_count, jb_count, slot_width)[
        None, :
    ]
    pair_rows = ladder.reshape(OI, OJ, ab_count)
    k_local = OJ // pair_devs
    own_k = lax.dynamic_slice_in_dim(pair_rows, lax.axis_index("pair") * k_local, k_local, 1)[None]
    cycle_local = cycle_integrals.reshape(k_local, irrep_total, slot_width, jb_count)
    shards = lax.all_gather(own_k, "virt", axis=0, tiled=True)
    shard_count = shards.shape[0]
    irrep_ids = jnp.arange(shard_count, dtype=jnp.int32) * ab_count // (slot_width * slot_width)
    chosen = jnp.take(cycle_local, irrep_ids, axis=1)
    amp_block = shards.reshape(shard_count, OI, k_local, a_count, slot_width)
    pieces = jnp.einsum("sikac,kscj->siaj", amp_block, chosen, preferred_element_type=jnp.float32)
    full_term = jnp.transpose(
        pieces.reshape(irrep_total, per_irrep, OI, a_count, jb_count), (2, 0, 1, 3, 4)
    )
    full_term = full_term.reshape(OI * group_width, jb_count)
    summed = lax.psum_scatter(full_term, "pair", scatter_dimension=0, tiled=True)
    cycle = (summed * keep_cols).astype(jnp.bfloat16)
    return (ladder, cycle)


def solution(mesh):
    placed = (P("virt", "pair"), P("virt", "pair"), P("pair", "virt"), P())
    return jax.shard_map(
        body,
        mesh=mesh,
        in_specs=placed,
        out_specs=(P(None, "virt"), P("pair", "virt")),
        check_vma=False,
    )
```

profile of v0, /device:TPU:1, one launch (start us, length us, event | category | flops | bytes accessed | tf_op | source)
XLA Modules:
  0.0 376.8 jit_solution(9450437816914688675)
XLA Ops:
  7.2 0.0 all-gather.4.cloned.1.call-start
  7.3 0.9 select_reduce_fusion
  8.2 0.1 convert_convert_fusion
  8.3 1.7 broadcast_multiply_fusion
  10.0 0.0 all-gather.4.cloned.1.call-update
  10.0 0.0 all-reduce.2.cloned.1.call-start
  10.1 109.0 %all-gather.4.cloned.1.call-done = bf16[512,16384]{1,0:T(8,128)(2,1)} async-done(((bf16[8,16384]{1,0:T(8,128)(2,1)}), bf16[512,16384]{1,0:T(8,128)(2,1)}) %all-gather.4.cloned.1.call-update) | async-done | bytes 16777232 | tf_op jit(solution)/shard_map/all_gather | solution.py:52
  119.1 18.0 %fusion.26 = f32[512,512]{1,0:T(8,128)} fusion(bf16[512,16384]{1,0:T(8,128)(2,1)} %all-gather.4.cloned.1.call-done, bf16[512,16384]{1,0:T(8,128)(2,1)} %param.5), kind=kOutput, calls=%fused_computation.87 | convolution fusion | flops 8589934592 | bytes 34603008 | tf_op jit(solution)/shard_map/dot_general | solution.py:51
  137.1 0.0 all-reduce.2.cloned.1.call-update
  137.1 0.0 all-gather.6.cloned.1.call-start
  137.2 0.1 select_reduce_fusion.1
  137.3 25.1 %all-reduce.2.cloned.1.call-done = f32[512,512]{1,0:T(8,128)} async-done(((f32[512,512]{1,0:T(8,128)}), f32[512,512]{1,0:T(8,128)}) %all-reduce.2.cloned.1.call-update) | async-done | bytes 1048592 | tf_op jit(solution)/shard_map/psum | solution.py:58
  162.4 1.3 multiply_convert_fusion.1
  163.8 0.8 constant_dynamic-slice_fusion
  164.6 0.0 reduce-scatter.2.cloned.1.call-start
  164.7 14.7 %gather_fusion = bf16[64,16,64,256]{3,2,1,0:T(8,128)(2,1)} fusion(bf16[16,8,64,256]{3,2,1,0:T(8,128)(2,1)} %bitcast.21, s32[1024]{0:T(1024)S(1)} %pad_clamp_fusion), kind=kCustom, calls=%fused_computation | custom fusion | bytes 67109120 | tf_op jit(solution)/shard_map/jit(_take)/gather | solution.py:70
  179.4 92.2 %all-gather.6.cloned.1.call-done = bf16[1024,16,512]{2,1,0:T(8,128)(2,1)} async-done(((bf16[16,16,512]{2,1,0:T(8,128)(2,1)}), bf16[1024,16,512]{2,1,0:T(8,128)(2,1)}) %all-gather.6.cloned.1.call-update) | async-done | bytes 16777232 | tf_op jit(solution)/shard_map/all_gather | solution.py:67
  271.6 41.3 %reshape.281 = bf16[64,16,16,8,64]{4,3,2,1,0:T(8,128)(2,1)} reshape(bf16[1024,16,512]{2,1,0:T(8,128)(2,1)} %all-gather.6.cloned.1.call-done) | data formatting | bytes 33554432 | tf_op jit(solution)/shard_map/reshape | solution.py:71
  312.9 25.9 %fusion = f32[64,16,8,256,1]{3,2,4,1,0:T(8,128)} fusion(bf16[64,16,16,8,64]{4,3,2,1,0:T(8,128)(2,1)} %reshape.281, bf16[64,16,64,256]{3,2,1,0:T(8,128)(2,1)} %gather_fusion, pred[64]{0:T(512)(128)(4,1)S(1)} %compare_and_fusion), kind=kOutput, calls=%fused_computation.1 | convolution fusion | flops 4311744512 | bytes 58720320 | tf_op jit(solution)/shard_map/sikac,kscj->siaj/dot_general | solution.py:72
  338.8 7.9 %copy.8 = f32[16,8,8,8,256]{4,3,2,1,0:T(8,128)} copy(f32[16,8,8,8,256]{4,3,0,2,1:T(8,128)} %bitcast.23) | data formatting | bytes 16777216 | tf_op jit(solution)/shard_map/transpose | solution.py:73
  346.7 0.0 reduce-scatter.2.cloned.1.call-update
  346.8 0.1 select_reduce_fusion.2
  346.9 19.5 %reduce-scatter.2.cloned.1.call-done = f32[4096,256]{1,0:T(8,128)} async-done(((f32[8192,256]{1,0:T(8,128)}), f32[4096,256]{1,0:T(8,128)}) %reduce-scatter.2.cloned.1.call-update) | async-done | bytes 4194320 | tf_op jit(solution)/shard_map/reduce_scatter | solution.py:77
  366.4 3.8 %multiply_convert_fusion = bf16[4096,256]{1,0:T(8,128)(2,1)} fusion(f32[4096,256]{1,0:T(8,128)} %reduce-scatter.2.cloned.1.call-done, f32[256]{0:T(256)S(1)} %compare_convert_fusion), kind=kLoop, calls=%fused_computation.6 | loop fusion | flops 2097152 | bytes 6292480 | tf_op jit(solution)/shard_map/convert_element_type | solution.py:78
  (13 shorter events, 0.2 us)
Async XLA Ops:
  7.2 111.9 %all-gather.4.cloned.1.call-start = ((), (), s32[]{:S(2)}) async-start(), calls=%async_computation.1 | async-start | bytes 17039360 | tf_op jit(solution)/shard_map/all_gather | solution.py:52
  10.0 127.2 %copy-start.1 = (s32[8]{0:T(128)S(1)}, s32[8]{0:T(128)}, u32[]{:S(2)}) copy-start(s32[8]{0:T(128)} %param.7) | copy-start | bytes 100
  10.0 152.4 %all-reduce.2.cloned.1.call-start = ((), (), s32[]{:S(2)}) async-start(), calls=%async_computation.2 | async-start | bytes 2097152 | tf_op jit(solution)/shard_map/psum | solution.py:58
  137.1 134.5 %all-gather.6.cloned.1.call-start = ((), (), s32[]{:S(2)}) async-start(), calls=%async_computation.4 | async-start | bytes 17039360 | tf_op jit(solution)/shard_map/all_gather | solution.py:67
  163.8 15.6 %copy-start = (bf16[512,512]{1,0:T(8,128)(2,1)}, bf16[512,512]{1,0:T(8,128)(2,1)S(1)}, u32[]{:S(2)}) copy-start(bf16[512,512]{1,0:T(8,128)(2,1)S(1)} %multiply_convert_fusion.1) | copy-start | bytes 1572868
  164.6 201.8 %reduce-scatter.2.cloned.1.call-start = ((), (), s32[]{:S(2)}) async-start(), calls=%async_computation.3 | async-start | bytes 12582912 | tf_op jit(solution)/shard_map/reduce_scatter | solution.py:77
Sparse Core Ops, SparseCore 0:
  11.4 107.5 all-gather.3
  137.2 25.1 all-reduce.1
  166.3 105.2 all-gather.5
  346.9 19.4 reduce-scatter.1
where the time goes:
time: 378 us; the launch traced here: 377 us
  waiting for transfers between devices  246 us (65%)
  local copies, waits for them, and re-layouts  64.7 us (17%)
  matrix products  43.9 us (12%)
  between operations  13.8 us (4%)
  other arithmetic  8.2 us (2%)
    all_gather x1, waiting for transfers between devices, body(): lax.all_gather(masked, 'virt', axis=0, tiled=True)  109 us
    all_gather x1, waiting for transfers between devices, body(): shards = lax.all_gather(own_k, 'virt', axis=0, tiled=True)  92.2 us
    reshape x1, local copies, waits for them, and re-layouts, body(): amp_block = shards.reshape(shard_count, OI, k_local, a_count, slot_width)  41.3 us
    dot_general x1, matrix products, body(): jnp.einsum('sikac,kscj->siaj', amp_block, chosen, preferred_element_type=...  25.9 us
    psum x1, waiting for transfers between devices, body(): ladder_total = lax.psum(partial_sums, 'pair')  25.1 us
    reduce_scatter x1, waiting for transfers between devices, body(): lax.psum_scatter(full_term, 'pair', scatter_dimension=0, tiled=True)  19.5 us
    dot_general x1, matrix products, body(): lax.dot_general(lax.all_gather(masked, 'virt', axis=0, tiled=True), integ...  18 us
    gather x1, local copies, waits for them, and re-layouts, body(): chosen = jnp.take(cycle_local, irrep_ids, axis=1)  14.7 us
  transfers between devices with their start and end apart: 4, of which 4 were waited for; matrix products, arithmetic and copies ran while one was open for 4% of the time, Pallas kernels for 0%

commit v1 on v0

v1 whole, which is shorter than its diff:
```python
import jax
import jax.numpy as jnp
from jax import lax
from jax.experimental import pallas as pl
from jax.experimental.pallas import tpu as pltpu
from jax.sharding import PartitionSpec as P

VH = 64
OI = 16
OJ = 32
F32 = jnp.float32
BF16 = jnp.bfloat16


def irrep_sizes(virt_count, irrep_of):
    irrep_ids = jnp.arange(virt_count.shape[0], dtype=jnp.int32)
    return jnp.sum(
        jnp.where(irrep_of[:, None] == irrep_ids[None, :], virt_count[None, :], 0), axis=1
    )


def pair_mask(virt_count, first_pos, length, slot_width):
    position = first_pos + jnp.arange(length, dtype=jnp.int32)
    irrep_of = position // (slot_width * slot_width)
    slot_one = position // slot_width % slot_width
    slot_two = position % slot_width
    irrep_size = irrep_sizes(virt_count, irrep_of)
    return ((slot_one < irrep_size) & (slot_two < irrep_size)).astype(F32)


def slot_mask(virt_count, first_pos, length, slot_width):
    position = (first_pos + jnp.arange(length, dtype=jnp.int32)) % (
        virt_count.shape[0] * slot_width
    )
    irrep_of = position // slot_width
    slot_ids = position % slot_width
    return (slot_ids < irrep_sizes(virt_count, irrep_of)).astype(F32)


def combine_kernel(own_ref, other_ref, keep_ref, ladder_ref, turned_ref, rows_ref, turn_ref):
    i_count = 8
    total = (own_ref[...] + other_ref[...]) * keep_ref[...]
    rounded = total.astype(BF16)
    ladder_ref[...] = rounded
    wide = rounded.astype(F32)
    for lane in range(4):
        rows_ref[lane] = wide[:, lane * 128 : (lane + 1) * 128]
    for kk in range(OJ // 2):
        for lane in range(4):
            even = rows_ref[lane, pl.ds(2 * kk, i_count, stride=OJ), :]
            odd = rows_ref[lane, pl.ds(2 * kk + 1, i_count, stride=OJ), :]
            turn_ref[kk, (2 * lane) * 8 : (2 * lane) * 8 + 8, :] = jnp.concatenate(
                [even[:, :VH], odd[:, :VH]], axis=1
            )
            turn_ref[kk, (2 * lane + 1) * 8 : (2 * lane + 1) * 8 + 8, :] = jnp.concatenate(
                [even[:, VH:], odd[:, VH:]], axis=1
            )
    for kk in range(OJ // 2):
        for i in range(i_count):
            turned_ref[i * 8 : (i + 1) * 8, kk * 128 : (kk + 1) * 128] = turn_ref[
                kk, pl.ds(i, 8, stride=8), :
            ].astype(BF16)


def combine(own, other, keep):
    rows, cols = own.shape
    return pl.pallas_call(
        combine_kernel,
        out_shape=(
            jax.ShapeDtypeStruct((rows, cols), BF16),
            jax.ShapeDtypeStruct((rows * cols // (OJ * VH), OJ * VH), BF16),
        ),
        scratch_shapes=[
            pltpu.VMEM((4, rows, 128), F32),
            pltpu.VMEM((OJ // 2, rows * cols // (OJ * VH), 128), F32),
        ],
        cost_estimate=pl.CostEstimate(flops=4 * rows * cols, bytes_accessed=12 * rows * cols, transcendentals=0),
    )(own, other, keep)


def cycle_kernel(half_ref, amp_own_ref, amp_other_ref, int_own_ref, int_other_ref, keep_ref, out_ref):
    rows = amp_own_ref.shape[0] * amp_own_ref.shape[1]
    depth = amp_own_ref.shape[2]
    width = int_own_ref.shape[3]
    total = jnp.dot(
        amp_own_ref[...].reshape(rows, depth), int_own_ref[...].reshape(depth, width),
        preferred_element_type=F32,
    ) + jnp.dot(
        amp_other_ref[...].reshape(rows, depth), int_other_ref[...].reshape(depth, width),
        preferred_element_type=F32,
    )
    total = (total * keep_ref[...]).astype(F32).reshape(8, 8, 8, width)
    for shard in range(8):
        out_ref[:, shard] = total[shard].astype(BF16)


def cycle_sum(half, gathered, int_own, int_other, keep):
    width = int_own.shape[3]
    depth = int_own.shape[0] * int_own.shape[2]
    grid_spec = pltpu.PrefetchScalarGridSpec(
        num_scalar_prefetch=1,
        grid=(8,),
        in_specs=[
            pl.BlockSpec((8, 64, depth), lambda h, half: (h, 0, half[0])),
            pl.BlockSpec((8, 64, depth), lambda h, half: (h, 0, 1 - half[0])),
            pl.BlockSpec((16, 1, 64, width), lambda h, half: (0, h, 0, 0)),
            pl.BlockSpec((16, 1, 64, width), lambda h, half: (0, h, 0, 0)),
            pl.BlockSpec((1, width), lambda h, half: (0, 0)),
        ],
        out_specs=pl.BlockSpec((8, 8, 8, width), lambda h, half: (0, h, 0, 0)),
    )
    return pl.pallas_call(
        cycle_kernel,
        out_shape=jax.ShapeDtypeStruct((8, 64, 8, width), BF16),
        grid_spec=grid_spec,
        compiler_params=pltpu.CompilerParams(
            dimension_semantics=("arbitrary",), vmem_limit_bytes=60 << 20
        ),
        cost_estimate=pl.CostEstimate(
            flops=2 * 4096 * 2048 * 256, bytes_accessed=27 << 20, transcendentals=0
        ),
    )(half, gathered, gathered, int_own, int_other, keep)


def body(amplitudes, integrals, cycle_integrals, virt_count):
    slot_width = VH
    ab_count = integrals.shape[0]
    cd_count = integrals.shape[1]
    jb_count = cycle_integrals.shape[1]
    pair = lax.axis_index("pair")
    virt = lax.axis_index("virt")
    swap = [(0, 1), (1, 0)]
    cycle_other = lax.ppermute(cycle_integrals, "pair", swap)
    masked = amplitudes * pair_mask(virt_count, pair * cd_count, cd_count, slot_width)[
        None, :
    ].astype(BF16)
    partial_sums = lax.dot_general(
        lax.all_gather(masked, "virt", axis=0, tiled=True),
        integrals,
        (((1,), (1,)), ((), ())),
        preferred_element_type=F32,
    )
    keep_pairs = pair_mask(virt_count, virt * ab_count, ab_count, slot_width)[None, :]
    half_rows = partial_sums.shape[0] // 2
    sent = lax.dynamic_slice_in_dim(partial_sums, (1 - pair) * half_rows, half_rows, 0)
    own = lax.dynamic_slice_in_dim(partial_sums, pair * half_rows, half_rows, 0)
    other = lax.ppermute(sent, "pair", swap)
    ladder_own, turned = combine(own, other, keep_pairs)
    gathered = lax.all_gather(turned, "virt", axis=0, tiled=True).reshape(64, 64, OJ * VH)
    ladder_other = lax.ppermute(ladder_own, "pair", swap)
    ladder = jnp.concatenate(
        [
            jnp.where(pair == 0, ladder_own, ladder_other),
            jnp.where(pair == 0, ladder_other, ladder_own),
        ],
        axis=0,
    )
    keep_cols = slot_mask(virt_count, virt * jb_count, jb_count, slot_width)[None, :]
    shape4 = (16, 8, slot_width, jb_count)
    cycle = cycle_sum(
        pair.astype(jnp.int32).reshape(1),
        gathered,
        cycle_integrals.reshape(shape4),
        cycle_other.reshape(shape4),
        keep_cols,
    )
    return (ladder, cycle.reshape(8 * 64 * 8, jb_count))


def solution(mesh):
    placed = (P("virt", "pair"), P("virt", "pair"), P("pair", "virt"), P())
    return jax.shard_map(
        body,
        mesh=mesh,
        in_specs=placed,
        out_specs=(P(None, "virt"), P("pair", "virt")),
        check_vma=False,
    )
```

time: 378 us -> 279 us (0.74)
  local copies, waits for them, and re-layouts: 64.7 us -> 1.68 us
  waiting for transfers between devices: 246 us -> 210 us
  Pallas kernels: 0 us -> 15.4 us
  matrix products: 43.9 us -> 29.9 us
    reshape x1 -> x0, local copies, waits for them, and re-layouts: 41.3 us -> none  [body(): amp_block = shards.reshape(shard_count, OI, k_local, a_count, slot_width)]
    dot_general x1 -> x0, matrix products: 25.9 us -> none  [body(): jnp.einsum('sikac,kscj->siaj', amp_block, chosen, preferred_element_type=...]
    psum x1 -> x0, waiting for transfers between devices: 25.1 us -> none  [body(): ladder_total = lax.psum(partial_sums, 'pair')]
    reduce_scatter x1 -> x0, waiting for transfers between devices: 19.5 us -> none  [body(): lax.psum_scatter(full_term, 'pair', scatter_dimension=0, tiled=True)]
    pallas_call x0 -> x2, Pallas kernels: none -> 15.4 us  [the longest x1 12.9 us: cycle_sum(): pl.pallas_call(cycle_kernel, out_shape=jax.ShapeDtypeStruct((8, 64, 8, wi...]
    gather x1 -> x0, local copies, waits for them, and re-layouts: 14.7 us -> none  [body(): chosen = jnp.take(cycle_local, irrep_ids, axis=1)]
    dot_general x1, matrix products: 18 us -> 29.9 us  [body(): lax.dot_general(lax.all_gather(masked, 'virt', axis=0, tiled=True), integ...]
    transpose x1 -> x0, local copies, waits for them, and re-layouts: 7.89 us -> none  [body(): jnp.transpose(pieces.reshape(irrep_total, per_irrep, OI, a_count, jb_coun...]
  transfers between devices with their start and end apart: 4 -> 5, of which waited for: 4 -> 4; matrix products, arithmetic and copies ran while one was open for 4% -> 1% of each run, Pallas kernels for 0% -> 0%
where the time goes in v1:
time: 279 us
  waiting for transfers between devices  210 us (75%)
  matrix products  29.9 us (11%)
  Pallas kernels  15.4 us (6%)
  between operations  14.1 us (5%)
  other arithmetic  6.01 us (2%)
    all_gather x1, waiting for transfers between devices, body(): lax.all_gather(masked, 'virt', axis=0, tiled=True)  109 us
    all_gather x1, waiting for transfers between devices, body(): lax.all_gather(turned, 'virt', axis=0, tiled=True).reshape(64, 64, OJ * VH)  95.1 us
    dot_general x1, matrix products, body(): lax.dot_general(lax.all_gather(masked, 'virt', axis=0, tiled=True), integ...  29.9 us
    pallas_call x1, Pallas kernels, cycle_sum(): pl.pallas_call(cycle_kernel, out_shape=jax.ShapeDtypeStruct((8, 64, 8, wi...  12.9 us
  transfers between devices with their start and end apart: 5, of which 4 were waited for; matrix products, arithmetic and copies ran while one was open for 1% of the time, Pallas kernels for 0%

profile of v1, /device:TPU:1, one launch (start us, length us, event | category | flops | bytes accessed | tf_op | source)
XLA Modules:
  0.0 278.9 jit_solution(17284824790796438942)
XLA Ops:
  7.2 0.0 all-gather.3.cloned.1.call-start
  7.3 0.9 select_reduce_fusion
  8.2 0.1 convert_convert_fusion
  8.3 1.7 broadcast_multiply_fusion
  10.0 0.0 all-gather.3.cloned.1.call-update
  10.0 0.0 all-gather.5.cloned.1.call-start
  10.1 109.0 %all-gather.3.cloned.1.call-done = bf16[512,16384]{1,0:T(8,128)(2,1)} async-done(((bf16[8,16384]{1,0:T(8,128)(2,1)}), bf16[512,16384]{1,0:T(8,128)(2,1)}) %all-gather.3.cloned.1.call-update) | async-done | bytes 16777232 | tf_op jit(solution)/shard_map/all_gather | solution.py:138
  119.1 29.9 %fusion.17 = f32[512,512]{1,0:T(8,128)S(1)} fusion(bf16[512,16384]{1,0:T(8,128)(2,1)} %all-gather.3.cloned.1.call-done, bf16[512,16384]{1,0:T(8,128)(2,1)} %param.5), kind=kOutput, calls=%fused_computation.72 | convolution fusion | flops 8589934592 | bytes 34603008 | tf_op jit(solution)/shard_map/dot_general | solution.py:137
  149.0 0.9 constant_dynamic-slice_fusion
  149.9 0.7 collective-permute-start
  150.6 0.1 select_reduce_fusion.1
  150.7 0.6 and_convert_fusion.keep_ref
  151.3 0.8 collective-permute-done.other_ref
  152.1 0.8 copy-done
  152.9 2.5 shard_map.59
  155.4 0.5 collective-permute-start.2
  155.9 0.2 collective-permute-start.1
  156.1 0.1 select_reduce_fusion.2
  156.2 0.6 compare_convert_fusion.keep_ref
  156.8 5.5 %collective-permute-done.1 = bf16[256,512]{1,0:T(8,128)(2,1)S(1)} collective-permute-done((bf16[256,512]{1,0:T(8,128)(2,1)}, bf16[256,512]{1,0:T(8,128)(2,1)S(1)}, u32[]{:S(2)}, u32[]{:S(2)}) %collective-permute-start.1) | collective-permute-done | bytes 262176 | tf_op jit(solution)/shard_map/ppermute | solution.py:150
  162.3 1.0 broadcast_select_fusion.1
  163.3 0.8 pad_maximum_fusion
  164.2 95.1 %all-gather.5.cloned.1.call-done = bf16[4096,2048]{1,0:T(8,128)(2,1)} async-done(((bf16[64,2048]{1,0:T(8,128)(2,1)}), bf16[4096,2048]{1,0:T(8,128)(2,1)}) %all-gather.5.cloned.1.call-update) | async-done | bytes 16777232 | tf_op jit(solution)/shard_map/all_gather | solution.py:149
  259.2 12.9 %shard_map.60 = bf16[8,64,8,256]{3,2,1,0:T(8,128)(2,1)} custom-call(s32[1]{0:T(128)} %bitcast.1.half_ref, bf16[64,64,2048]{2,1,0:T(8,128)(2,1)} %bitcast.9, bf16[64,64,2048]{2,1,0:T(8,128)(2,1)} %bitcast.10, bf16[16,8,64,256]{3,2,1,0:T(8,128)(2,1)} %bitcast.11, bf16[16,8,64,256]{3,2,1,0:T(8,128)(2,1)} %bitcast.4.int_other_ref, ...), custom_call_target="tpu_custom_call" | custom-call | flops 4294967296 | bytes 28311552 | tf_op jit(solution)/shard_map/pallas_call | solution.py:112
  (8 shorter events, 0.1 us)
Async XLA Ops:
  7.2 111.9 %all-gather.3.cloned.1.call-start = ((), (), s32[]{:S(2)}) async-start(), calls=%async_computation | async-start | bytes 17039360 | tf_op jit(solution)/shard_map/all_gather | solution.py:138
  10.0 249.2 %all-gather.5.cloned.1.call-start = ((), (), s32[]{:S(2)}) async-start(), calls=%async_computation.1 | async-start | bytes 17039360 | tf_op jit(solution)/shard_map/all_gather | solution.py:149
  10.1 140.5 %copy-start.1 = (s32[8]{0:T(128)S(1)}, s32[8]{0:T(128)}, u32[]{:S(2)}) copy-start(s32[8]{0:T(128)} %param.7) | copy-start | bytes 100
  149.9 2.2 collective-permute-start
  152.1 0.8 copy-start
  155.4 8.7 %collective-permute-start.2 = (bf16[8192,256]{1,0:T(8,128)(2,1)}, bf16[8192,256]{1,0:T(8,128)(2,1)}, u32[]{:S(2)}, u32[]{:S(2)}) collective-permute-start(bf16[8192,256]{1,0:T(8,128)(2,1)} %param.6), channel_id=1, source_target_pairs={{0,64},{64,0},{1,65},{65,1},{2,66},{66,2},{3,67},{67,3},{4,68},{68... | collective-permute-start | bytes 12582920 | tf_op jit(solution)/shard_map/ppermute | solution.py:133
  155.9 6.4 %collective-permute-start.1 = (bf16[256,512]{1,0:T(8,128)(2,1)}, bf16[256,512]{1,0:T(8,128)(2,1)S(1)}, u32[]{:S(2)}, u32[]{:S(2)}) collective-permute-start(bf16[256,512]{1,0:T(8,128)(2,1)} %get-tuple-element.4), channel_id=1, source_target_pairs={{0,64},{64,0},{1,65},{65,1},{2,66},{66,2},{3,67},{67,3},{4,68},{68... | collective-permute-start | bytes 786440 | tf_op jit(solution)/shard_map/ppermute | solution.py:150
Sparse Core Ops, SparseCore 0:
  11.5 107.5 all-gather.2
  155.5 103.6 all-gather.4

commit v2 on v1

v2 whole, which is shorter than its diff:
```python
import jax
import jax.numpy as jnp
from jax import lax
from jax.experimental import pallas as pl
from jax.experimental.pallas import tpu as pltpu
from jax.sharding import PartitionSpec as P

VH = 64
OI = 16
OJ = 32
F32 = jnp.float32
BF16 = jnp.bfloat16


def irrep_sizes(virt_count, irrep_of):
    irrep_ids = jnp.arange(virt_count.shape[0], dtype=jnp.int32)
    return jnp.sum(
        jnp.where(irrep_of[:, None] == irrep_ids[None, :], virt_count[None, :], 0), axis=1
    )


def pair_mask(virt_count, first_pos, length, slot_width):
    position = first_pos + jnp.arange(length, dtype=jnp.int32)
    irrep_of = position // (slot_width * slot_width)
    slot_one = position // slot_width % slot_width
    slot_two = position % slot_width
    irrep_size = irrep_sizes(virt_count, irrep_of)
    return ((slot_one < irrep_size) & (slot_two < irrep_size)).astype(F32)


def slot_mask(virt_count, first_pos, length, slot_width):
    position = (first_pos + jnp.arange(length, dtype=jnp.int32)) % (
        virt_count.shape[0] * slot_width
    )
    irrep_of = position // slot_width
    slot_ids = position % slot_width
    return (slot_ids < irrep_sizes(virt_count, irrep_of)).astype(F32)


SHARDS = 64
SWAP = [(0, 1), (1, 0)]


NT = (((1,), (1,)), ((), ()))
DEPTH = 2048


def ladder_kernel(pair_ref, amp_ref, weight_ref, own_ref, sent_ref, total_ref):
    step = pl.program_id(0)
    part = lax.dot_general(amp_ref[...], weight_ref[...], NT, preferred_element_type=F32)

    @pl.when(step == 0)
    def _():
        total_ref[...] = part

    @pl.when(step > 0)
    def _():
        total_ref[...] += part

    @pl.when(step == pl.num_programs(0) - 1)
    def _():
        half = own_ref.shape[0]
        own_ref[...] = total_ref[pl.ds(pl.multiple_of(pair_ref[0] * half, half), half)]
        sent_ref[...] = total_ref[pl.ds(pl.multiple_of((1 - pair_ref[0]) * half, half), half)]


def ladder_sums(pair, amps, integrals):
    rows, depth = amps.shape
    cols = integrals.shape[0]
    half = jax.ShapeDtypeStruct((rows // 2, cols), F32)
    half_spec = pl.BlockSpec((rows // 2, cols), lambda s, p: (0, 0))
    grid_spec = pltpu.PrefetchScalarGridSpec(
        num_scalar_prefetch=1,
        grid=(depth // DEPTH,),
        in_specs=[
            pl.BlockSpec((rows, DEPTH), lambda s, p: (0, s)),
            pl.BlockSpec((cols, DEPTH), lambda s, p: (0, s)),
        ],
        out_specs=[half_spec, half_spec],
        scratch_shapes=[pltpu.VMEM((rows, cols), F32)],
    )
    return pl.pallas_call(
        ladder_kernel,
        out_shape=[half, half],
        grid_spec=grid_spec,
        compiler_params=pltpu.CompilerParams(
            dimension_semantics=("arbitrary",), vmem_limit_bytes=60 << 20
        ),
        cost_estimate=pl.CostEstimate(
            flops=2 * rows * cols * depth, bytes_accessed=36 << 20, transcendentals=0
        ),
    )(pair, amps, integrals)


def combine_kernel(own_ref, other_ref, keep_ref, ladder_ref, *refs):
    turned_ref, rows_ref, turn_ref = refs
    i_count = 8
    total = (own_ref[...] + other_ref[...]) * keep_ref[...]
    rounded = total.astype(BF16)
    ladder_ref[...] = rounded
    wide = rounded.astype(F32)
    for lane in range(4):
        rows_ref[lane] = wide[:, lane * 128 : (lane + 1) * 128]
    for kk in range(OJ // 2):
        for lane in range(4):
            even = rows_ref[lane, pl.ds(2 * kk, i_count, stride=OJ), :]
            odd = rows_ref[lane, pl.ds(2 * kk + 1, i_count, stride=OJ), :]
            turn_ref[kk, (2 * lane) * 8 : (2 * lane) * 8 + 8, :] = jnp.concatenate(
                [even[:, :VH], odd[:, :VH]], axis=1
            )
            turn_ref[kk, (2 * lane + 1) * 8 : (2 * lane + 1) * 8 + 8, :] = jnp.concatenate(
                [even[:, VH:], odd[:, VH:]], axis=1
            )
    for kk in range(OJ // 2):
        for i in range(i_count):
            turned_ref[i * 8 : i * 8 + 8, kk * 128 : (kk + 1) * 128] = turn_ref[
                kk, pl.ds(i, 8, stride=8), :
            ].astype(BF16)


def combine(own, other, keep):
    rows, cols = own.shape
    return pl.pallas_call(
        combine_kernel,
        out_shape=[jax.ShapeDtypeStruct((rows, cols), BF16)]
        + [jax.ShapeDtypeStruct((64, OJ * VH), BF16)],
        scratch_shapes=[
            pltpu.VMEM((4, rows, 128), F32),
            pltpu.VMEM((OJ // 2, rows * cols // (OJ * VH), 128), F32),
        ],
        cost_estimate=pl.CostEstimate(
            flops=4 * rows * cols, bytes_accessed=12 * rows * cols, transcendentals=0
        ),
    )(own, other, keep)


AHEAD = 2


def fetch_integrals(h, pair, int_own_ref, int_other_ref, int_ref, int_sem):
    for part, source in enumerate((int_own_ref, int_other_ref)):
        first = (pair if part == 0 else 1 - pair) * 16
        pltpu.make_async_copy(
            source.at[:, pl.ds(h, 1)],
            int_ref.at[pl.ds(first, 16), pl.ds(h, 1)],
            int_sem.at[h],
        ).start()


def cycle_kernel(pair_ref, amps_ref, int_own_ref, int_other_ref, keep_ref, out_ref, *scratch):
    amp_ref, int_ref, amp_sem, int_sem = scratch
    keep = keep_ref[...]
    width = keep.shape[1]
    deep = OJ * VH

    def fetch(h):
        fetch_integrals(h, pair_ref[0], int_own_ref, int_other_ref, int_ref, int_sem)
        shards = pl.ds(h * 8, 8)
        pltpu.make_async_copy(amps_ref.at[shards], amp_ref.at[shards], amp_sem.at[h]).start()

    for h in range(AHEAD):
        fetch(h)

    @pl.loop(0, 8)
    def _(h):
        @pl.when(h + AHEAD < 8)
        def _():
            fetch(h + AHEAD)

        ints = int_ref.at[:, pl.ds(h, 1)]
        amps = amp_ref.at[pl.ds(h * 8, 8)]
        pltpu.make_async_copy(ints, ints, int_sem.at[h]).wait()
        pltpu.make_async_copy(amps, amps, amp_sem.at[h]).wait()
        left = amps[...].reshape(8 * 64, deep)
        right = ints[...].reshape(deep, width)
        total = jnp.dot(left, right, preferred_element_type=F32) * keep
        total = total.reshape(8, 8, 8, width)
        for i in range(8):
            out_ref[i, pl.ds(h * 8, 8)] = total[:, i].astype(BF16)


ANYWHERE = pl.BlockSpec(memory_space=pl.ANY)
SCALARS = pl.BlockSpec(memory_space=pltpu.SMEM)
LOCAL = pl.BlockSpec(memory_space=pltpu.VMEM)


def cycle_sum(pair, amps, int_own, int_other, keep):
    width = int_own.shape[3]
    return pl.pallas_call(
        cycle_kernel,
        out_shape=jax.ShapeDtypeStruct((8, SHARDS, 8, width), BF16),
        in_specs=[SCALARS] + [ANYWHERE] * 3 + [LOCAL],
        out_specs=LOCAL,
        scratch_shapes=[
            pltpu.VMEM((SHARDS, 64, OJ * VH), BF16),
            pltpu.VMEM((OJ, 8, VH, width), BF16),
            pltpu.SemaphoreType.DMA((8,)),
            pltpu.SemaphoreType.DMA((8,)),
        ],
        compiler_params=pltpu.CompilerParams(vmem_limit_bytes=60 << 20),
        cost_estimate=pl.CostEstimate(
            flops=2 * 4096 * 2048 * 256, bytes_accessed=27 << 20, transcendentals=0
        ),
    )(pair, amps, int_own, int_other, keep)


def body(amplitudes, integrals, cycle_integrals, virt_count):
    slot_width = VH
    ab_count = integrals.shape[0]
    cd_count = integrals.shape[1]
    jb_count = cycle_integrals.shape[1]
    pair = lax.axis_index("pair")
    virt = lax.axis_index("virt")
    pair_id = pair.astype(jnp.int32).reshape(1)
    cycle_other = lax.ppermute(cycle_integrals, "pair", SWAP)
    masked = amplitudes * pair_mask(virt_count, pair * cd_count, cd_count, slot_width)[
        None, :
    ].astype(BF16)
    amps = lax.all_gather(masked, "virt", axis=0, tiled=True)
    own, sent = ladder_sums(pair_id, amps, integrals)
    keep_pairs = pair_mask(virt_count, virt * ab_count, ab_count, slot_width)[None, :]
    other = lax.ppermute(sent, "pair", SWAP)
    ladder_own, turned = combine(own, other, keep_pairs)
    amps = lax.all_gather(turned, "virt", axis=0, tiled=True).reshape(SHARDS, 64, OJ * VH)
    ladder_other = lax.ppermute(ladder_own, "pair", SWAP)
    ladder = jnp.concatenate(
        [
            jnp.where(pair == 0, ladder_own, ladder_other),
            jnp.where(pair == 0, ladder_other, ladder_own),
        ],
        axis=0,
    )
    keep_cols = slot_mask(virt_count, virt * jb_count, jb_count, slot_width)[None, :]
    shape4 = (16, 8, slot_width, jb_count)
    cycle = cycle_sum(
        pair_id, amps, cycle_integrals.reshape(shape4), cycle_other.reshape(shape4), keep_cols
    )
    return (ladder, cycle.reshape(8 * SHARDS * 8, jb_count))


def solution(mesh):
    placed = (P("virt", "pair"), P("virt", "pair"), P("pair", "virt"), P())
    return jax.shard_map(
        body,
        mesh=mesh,
        in_specs=placed,
        out_specs=(P(None, "virt"), P("pair", "virt")),
        check_vma=False,
    )
```

time: 279 us -> 265 us (0.950)
  matrix products: 29.9 us -> 0 us
  Pallas kernels: 15.4 us -> 31.3 us
    dot_general x1 -> x0, matrix products: 29.9 us -> none  [body(): lax.dot_general(lax.all_gather(masked, 'virt', axis=0, tiled=True), integ...]
    pallas_call x2 -> x3, Pallas kernels: 15.4 us -> 31.3 us  [the longest x1 17.3 us: ladder_sums(): pl.pallas_call(ladder_kernel, out_shape=[half, half], grid_spec=grid_spec...]
where the time goes in v2:
time: 265 us; the launch traced here: 264 us
  waiting for transfers between devices  211 us (80%)
  Pallas kernels  31.3 us (12%)
  between operations  14.1 us (5%)
  other arithmetic  5.98 us (2%)
    all_gather x1, waiting for transfers between devices, body(): amps = lax.all_gather(masked, 'virt', axis=0, tiled=True)  109 us
    all_gather x1, waiting for transfers between devices, body(): lax.all_gather(turned, 'virt', axis=0, tiled=True)  95.1 us
    pallas_call x1, Pallas kernels, ladder_sums(): pl.pallas_call(ladder_kernel, out_shape=[half, half], grid_spec=grid_spec...  17.3 us
    pallas_call x1, Pallas kernels, cycle_sum(): pl.pallas_call(cycle_kernel, out_shape=jax.ShapeDtypeStruct((8, SHARDS, 8...  11.5 us
    ppermute x1, waiting for transfers between devices, body(): ladder_other = lax.ppermute(ladder_own, 'pair', SWAP)  5.53 us
  transfers between devices with their start and end apart: 5, of which 4 were waited for; matrix products, arithmetic and copies ran while one was open for 1% of the time, Pallas kernels for 0%

profile of v2, /device:TPU:1, one launch (start us, length us, event | category | flops | bytes accessed | tf_op | source)
XLA Modules:
  0.0 264.3 jit_solution(2108305022707101450)
XLA Ops:
  7.2 0.0 all-gather.3.cloned.1.call-start
  7.3 0.9 select_reduce_fusion
  8.2 0.1 convert_convert_fusion
  8.3 1.7 broadcast_multiply_fusion
  10.0 0.0 all-gather.3.cloned.1.call-update
  10.0 0.0 all-gather.5.cloned.1.call-start
  10.0 109.0 %all-gather.3.cloned.1.call-done.amp_ref = bf16[512,16384]{1,0:T(8,128)(2,1)} async-done(((bf16[8,16384]{1,0:T(8,128)(2,1)}), bf16[512,16384]{1,0:T(8,128)(2,1)}) %all-gather.3.cloned.1.call-update) | async-done | bytes 16777232 | tf_op jit(solution)/shard_map/all_gather | solution.py:219
  119.1 17.3 %shard_map.59 = (f32[256,512]{1,0:T(8,128)}, f32[256,512]{1,0:T(8,128)}) custom-call(s32[1]{0:T(128)} %bitcast.pair_ref, bf16[512,16384]{1,0:T(8,128)(2,1)} %all-gather.3.cloned.1.call-done.amp_ref, bf16[512,16384]{1,0:T(8,128)(2,1)} %weight_ref.1), custom_call_target="tpu_custom_call" | custom-call | flops 8589934592 | bytes 37748736 | tf_op jit(solution)/shard_map/pallas_call | solution.py:82
  136.4 0.7 collective-permute-start
  137.1 0.1 select_reduce_fusion.1
  137.2 0.6 and_convert_fusion.keep_ref
  137.8 1.0 collective-permute-done.other_ref
  138.9 0.8 copy-done
  139.6 2.5 shard_map.60
  142.1 0.0 all-gather.5.cloned.1.call-update
  142.1 0.5 collective-permute-start.2
  142.6 0.2 collective-permute-start.1
  142.8 0.1 select_reduce_fusion.2
  142.9 0.6 compare_convert_fusion.keep_ref
  143.5 5.5 %collective-permute-done.1 = bf16[256,512]{1,0:T(8,128)(2,1)S(1)} collective-permute-done((bf16[256,512]{1,0:T(8,128)(2,1)}, bf16[256,512]{1,0:T(8,128)(2,1)S(1)}, u32[]{:S(2)}, u32[]{:S(2)}) %collective-permute-start.1) | collective-permute-done | bytes 262176 | tf_op jit(solution)/shard_map/ppermute | solution.py:225
  149.0 1.0 broadcast_select_fusion.1
  150.0 0.8 pad_maximum_fusion
  150.9 95.1 %all-gather.5.cloned.1.call-done = bf16[4096,2048]{1,0:T(8,128)(2,1)} async-done(((bf16[64,2048]{1,0:T(8,128)(2,1)}), bf16[4096,2048]{1,0:T(8,128)(2,1)}) %all-gather.5.cloned.1.call-update) | async-done | bytes 16777232 | tf_op jit(solution)/shard_map/all_gather | solution.py:224
  245.9 11.5 %shard_map.61 = bf16[8,64,8,256]{3,2,1,0:T(8,128)(2,1)} custom-call(s32[1]{0:T(128)} %bitcast.pair_ref, bf16[64,64,2048]{2,1,0:T(8,128)(2,1)} %bitcast.7, bf16[16,8,64,256]{3,2,1,0:T(8,128)(2,1)} %bitcast.8, bf16[16,8,64,256]{3,2,1,0:T(8,128)(2,1)} %bitcast.4.int_other_ref, f32[1,256]{1,0:T(1,128)} %compare_convert_fusion.keep_ref), custom_call_target="tpu_custom_call" | custom-call | flops 4294967296 | bytes 28311552 | tf_op jit(solution)/shard_map/pallas_call | solution.py:189
  (7 shorter events, 0.1 us)
Async XLA Ops:
  7.2 111.9 %all-gather.3.cloned.1.call-start = ((), (), s32[]{:S(2)}) async-start(), calls=%async_computation | async-start | bytes 17039360 | tf_op jit(solution)/shard_map/all_gather | solution.py:219
  10.0 235.9 %all-gather.5.cloned.1.call-start = ((), (), s32[]{:S(2)}) async-start(), calls=%async_computation.1 | async-start | bytes 17039360 | tf_op jit(solution)/shard_map/all_gather | solution.py:224
  119.1 18.0 %copy-start.1 = (s32[8]{0:T(128)S(1)}, s32[8]{0:T(128)}, u32[]{:S(2)}) copy-start(s32[8]{0:T(128)} %param.7) | copy-start | bytes 100
  136.4 2.4 collective-permute-start
  138.9 0.8 copy-start
  142.1 8.7 %collective-permute-start.2 = (bf16[8192,256]{1,0:T(8,128)(2,1)}, bf16[8192,256]{1,0:T(8,128)(2,1)}, u32[]{:S(2)}, u32[]{:S(2)}) collective-permute-start(bf16[8192,256]{1,0:T(8,128)(2,1)} %param.6), channel_id=1, source_target_pairs={{0,64},{64,0},{1,65},{65,1},{2,66},{66,2},{3,67},{67,3},{4,68},{68... | collective-permute-start | bytes 12582920 | tf_op jit(solution)/shard_map/ppermute | solution.py:215
  142.6 6.4 %collective-permute-start.1 = (bf16[256,512]{1,0:T(8,128)(2,1)}, bf16[256,512]{1,0:T(8,128)(2,1)S(1)}, u32[]{:S(2)}, u32[]{:S(2)}) collective-permute-start(bf16[256,512]{1,0:T(8,128)(2,1)} %get-tuple-element.8), channel_id=1, source_target_pairs={{0,64},{64,0},{1,65},{65,1},{2,66},{66,2},{3,67},{67,3},{4,68},{68... | collective-permute-start | bytes 786440 | tf_op jit(solution)/shard_map/ppermute | solution.py:225
Sparse Core Ops, SparseCore 0:
  11.5 107.5 all-gather.2
  142.3 103.6 all-gather.4
